TPU v7x, 32 devices: a whole 2x2x4 slice. The times are simulated.
32 devices in a mesh: dp: 8 (over y, x, core), seq: 4 (over z).
Axes of the slice: x: 2, y: 2, z: 4, core: 2. Of those that a mesh axis runs over, the one named last changes fastest.
Arguments:
- hidden_in: bfloat16 [8, 2048, 1024], P('dp', 'seq'), may hold values from -6 to 6
- doc_lengths: int32 [8, 8], P('dp'), may hold values from 1 to 1024, 2048 in all within a row
- ln1_gain: float32 [1024], replicated, may hold values from 0.1 to 1.9
- ln1_bias: float32 [1024], replicated, may hold values from -1.75 to 1.75
- ln2_gain: float32 [1024], replicated, may hold values from 0.1 to 1.9
- ln2_bias: float32 [1024], replicated, may hold values from -1.75 to 1.75
- qkv_weight: bfloat16 [1024, 3072], replicated, may hold values from -0.1875 to 0.1875
- qkv_bias: float32 [3072], replicated, may hold values from -1.75 to 1.75
- dense_weight: bfloat16 [1024, 1024], replicated, may hold values from -0.75 to 0.75
- dense_bias: float32 [1024], replicated, may hold values from -1.75 to 1.75
- fc_in_weight: bfloat16 [1024, 4096], replicated, may hold values from -0.1875 to 0.1875
- fc_in_bias: float32 [4096], replicated, may hold values from -1.75 to 1.75
- fc_out_weight: bfloat16 [4096, 1024], replicated, may hold values from -0.09375 to 0.09375
- fc_out_bias: float32 [1024], replicated, may hold values from -1.75 to 1.75
- out_grad: bfloat16 [8, 2048, 1024], P('dp', 'seq'), may hold values from -8 to 8
Outputs:
- hidden_out: bfloat16 [8, 2048, 1024], P('dp', 'seq')
- grad_in: float32 [8, 2048, 1024], P('dp', 'seq')
- grad_ln1_gain: float32 [1024], P(('dp', 'seq'))
- grad_ln1_bias: float32 [1024], P(('dp', 'seq'))
- grad_ln2_gain: float32 [1024], P(('dp', 'seq'))
- grad_ln2_bias: float32 [1024], P(('dp', 'seq'))
- grad_qkv_weight: float32 [1024, 3072], P(('dp', 'seq'))
- grad_qkv_bias: float32 [3072], P(('dp', 'seq'))
- grad_dense_weight: float32 [1024, 1024], P(('dp', 'seq'))
- grad_dense_bias: float32 [1024], P(('dp', 'seq'))
- grad_fc_in_weight: float32 [1024, 4096], P(('dp', 'seq'))
- grad_fc_in_bias: float32 [4096], P(('dp', 'seq'))
- grad_fc_out_weight: float32 [4096, 1024], P(('dp', 'seq'))
- grad_fc_out_bias: float32 [1024], P(('dp', 'seq'))
Inputs may be any that keep to these rules, and one draw needn't show every extreme that they name: `doc_lengths`: each row sums to 2048; its last entry is the padding document.
All inputs are finite; a program needn't handle non-finite values.
Results may differ from a plain program's by a relative error of at most 0.0097.
Values may be sent and summed in bfloat16 or wider, within the bound.
A program may use at most 256 MiB of HBM per device.

v0:
```python
import jax
import jax.numpy as jnp
from jax import lax
from jax.sharding import PartitionSpec as P

HEADS = 16
HEAD = 64
ROT = 16
epsilon = 1e-05
masked_score = -1e30


def layout(lengths, positions):
    doc_ends = jnp.cumsum(lengths, axis=1)
    starts = doc_ends - lengths
    segment = jnp.sum((positions[None, :, None] >= doc_ends[:, None, :]).astype(jnp.int32), axis=2)
    belongs = segment[:, :, None] == jnp.arange(lengths.shape[1], dtype=jnp.int32)[None, None, :]
    doc_start = jnp.sum(jnp.where(belongs, starts[:, None, :], 0), axis=2)
    return (segment, positions[None, :] - doc_start)


def standardize(values):
    average = jnp.mean(values, axis=-1, keepdims=True)
    centered = values - average
    variance = jnp.mean(centered * centered, axis=-1, keepdims=True)
    inv_std = lax.rsqrt(variance + epsilon)
    return (centered * inv_std, inv_std)


def norm_back(d_normed, unit, inv_std, gain):
    gain_grad = jnp.sum(d_normed * unit, axis=0)
    bias_grad = jnp.sum(d_normed, axis=0)
    d_unit = d_normed * gain
    d_input = inv_std * (
        d_unit
        - jnp.mean(d_unit, axis=-1, keepdims=True)
        - unit * jnp.mean(d_unit * unit, axis=-1, keepdims=True)
    )
    return (d_input, gain_grad, bias_grad)


def rotary_tables(positions):
    half_rot = ROT // 2
    inverse = 10000.0 ** (-(2.0 * jnp.arange(half_rot, dtype=jnp.float32)) / ROT)
    angle = positions.astype(jnp.float32)[:, None] * inverse[None, :]
    return (jnp.cos(angle)[:, None, None, :], jnp.sin(angle)[:, None, None, :])


def rotate(packed, cosine, sine_part):
    half_rot = cosine.shape[-1]
    first_half = packed[..., :half_rot]
    second_half = packed[..., half_rot : 2 * half_rot]
    turned = jnp.concatenate(
        [
            first_half * cosine - second_half * sine_part,
            second_half * cosine + first_half * sine_part,
            packed[..., 2 * half_rot :],
        ],
        axis=-1,
    )
    return jnp.concatenate([turned[..., :2, :], packed[..., 2:, :]], axis=-2)


def exact_gelu(values):
    return jax.nn.gelu(values, approximate=False)


def transpose_dot(left, right):
    return lax.dot_general(
        left, right, (((0,), (0,)), ((), ())), preferred_element_type=jnp.float32
    )


def masked_scores(queries, keys_all, seg_full, first_row, last_row, score_scale):
    scores = (
        jnp.einsum(
            "bqhd,bkhd->bhqk",
            queries[:, first_row:last_row],
            keys_all[:, :last_row],
            preferred_element_type=jnp.float32,
        )
        * score_scale
    )
    query_index = jnp.arange(first_row, last_row, dtype=jnp.int32)
    key_index = jnp.arange(last_row, dtype=jnp.int32)
    allowed = (seg_full[:, first_row:last_row, None] == seg_full[:, None, :last_row]) & (
        query_index[None, :, None] >= key_index[None, None, :]
    )
    return jnp.where(allowed[:, None], scores, masked_score)


def shards(
    hidden_in,
    doc_lengths,
    ln1_gain,
    ln1_bias,
    ln2_gain,
    ln2_bias,
    qkv_weight,
    qkv_bias,
    dense_weight,
    dense_bias,
    fc_in_weight,
    fc_in_bias,
    fc_out_weight,
    fc_out_bias,
    out_grad,
):
    seqs_here, local_len, model_width = hidden_in.shape
    seq_parts = lax.axis_size("seq")
    full_len = local_len * seq_parts
    heads_here = HEADS // seq_parts
    row_count = seqs_here * local_len
    score_scale = HEAD ** (-0.5)
    block_rows = min(512, full_len)
    local_pos = lax.axis_index("seq") * local_len + jnp.arange(local_len, dtype=jnp.int32)
    seg_local, pos_local = layout(doc_lengths, local_pos)
    live_rows = (seg_local < doc_lengths.shape[1] - 1).astype(jnp.float32).reshape(row_count, 1)
    input_f32 = hidden_in.astype(jnp.float32).reshape(row_count, model_width)
    unit_attn, inv_attn = standardize(input_f32)
    unit_mlp, inv_mlp = standardize(input_f32)
    normed_attn = (unit_attn * ln1_gain + ln1_bias).astype(jnp.bfloat16)
    normed_mlp = (unit_mlp * ln2_gain + ln2_bias).astype(jnp.bfloat16)
    qkv_f32 = jnp.dot(normed_attn, qkv_weight, preferred_element_type=jnp.float32) + qkv_bias
    shaped = qkv_f32.reshape(row_count, HEADS, 3, HEAD)
    cosine, sine_part = rotary_tables(pos_local.reshape(row_count))
    turned = (
        rotate(shaped, cosine, sine_part)
        .astype(jnp.bfloat16)
        .reshape(seqs_here, local_len, 3 * model_width)
    )
    head_side = lax.all_to_all(turned, "seq", split_axis=2, concat_axis=1, tiled=True).reshape(
        seqs_here, full_len, heads_here, 3, HEAD
    )
    queries = head_side[:, :, :, 0]
    keys_all = head_side[:, :, :, 1]
    values_all = head_side[:, :, :, 2]
    seg_full, _ = layout(doc_lengths, jnp.arange(full_len, dtype=jnp.int32))
    context_parts = []
    lse_parts = []
    for first_row in range(0, full_len, block_rows):
        last_row = first_row + block_rows
        scores = masked_scores(queries, keys_all, seg_full, first_row, last_row, score_scale)
        peak_score = jnp.max(scores, axis=-1, keepdims=True)
        exponentials = jnp.exp(scores - peak_score)
        weight_sum = jnp.sum(exponentials, axis=-1, keepdims=True)
        probability = exponentials / weight_sum
        lse_parts.append(peak_score[..., 0] + jnp.log(weight_sum[..., 0]))
        context_parts.append(
            jnp.einsum(
                "bhqk,bkhd->bqhd",
                probability.astype(jnp.bfloat16),
                values_all[:, :last_row],
                preferred_element_type=jnp.float32,
            )
        )
    context_heads = (
        jnp.concatenate(context_parts, axis=1)
        .astype(jnp.bfloat16)
        .reshape(seqs_here, full_len, heads_here * HEAD)
    )
    log_sums = jnp.concatenate(lse_parts, axis=2)
    context_tok = lax.all_to_all(
        context_heads, "seq", split_axis=1, concat_axis=2, tiled=True
    ).reshape(row_count, model_width)
    attn_branch = (
        jnp.dot(context_tok, dense_weight, preferred_element_type=jnp.float32) + dense_bias
    )
    pre_act = jnp.dot(normed_mlp, fc_in_weight, preferred_element_type=jnp.float32) + fc_in_bias
    activated, gelu_pull = jax.vjp(exact_gelu, pre_act)
    act_low = activated.astype(jnp.bfloat16)
    mlp_branch = jnp.dot(act_low, fc_out_weight, preferred_element_type=jnp.float32) + fc_out_bias
    hidden_out = (
        (input_f32 + attn_branch + mlp_branch)
        .astype(jnp.bfloat16)
        .reshape(seqs_here, local_len, model_width)
    )
    gradient = out_grad.astype(jnp.float32).reshape(row_count, model_width) * live_rows
    grad_low = gradient.astype(jnp.bfloat16)
    g_dense_w = transpose_dot(context_tok, grad_low)
    g_dense_b = jnp.sum(gradient, axis=0)
    d_context = jnp.dot(grad_low, dense_weight.T, preferred_element_type=jnp.float32).astype(
        jnp.bfloat16
    )
    d_context_heads = lax.all_to_all(
        d_context.reshape(seqs_here, local_len, model_width),
        "seq",
        split_axis=2,
        concat_axis=1,
        tiled=True,
    ).reshape(seqs_here, full_len, heads_here, HEAD)
    g_out_w = transpose_dot(act_low, grad_low)
    g_out_b = jnp.sum(gradient, axis=0)
    d_act = jnp.dot(grad_low, fc_out_weight.T, preferred_element_type=jnp.float32)
    d_pre = gelu_pull(d_act)[0].astype(jnp.bfloat16)
    g_in_w = transpose_dot(normed_mlp, d_pre)
    g_in_b = jnp.sum(d_pre.astype(jnp.float32), axis=0)
    d_mlp_in = jnp.dot(d_pre, fc_in_weight.T, preferred_element_type=jnp.float32)
    d_keys = jnp.zeros((seqs_here, full_len, heads_here, HEAD), jnp.float32)
    d_values = jnp.zeros((seqs_here, full_len, heads_here, HEAD), jnp.float32)
    d_query_parts = []
    for first_row in range(0, full_len, block_rows):
        last_row = first_row + block_rows
        scores = masked_scores(queries, keys_all, seg_full, first_row, last_row, score_scale)
        probability = jnp.exp(scores - log_sums[:, :, first_row:last_row, None])
        grad_rows = d_context_heads[:, first_row:last_row]
        d_values = d_values.at[:, :last_row].add(
            jnp.einsum(
                "bhqk,bqhd->bkhd",
                probability.astype(jnp.bfloat16),
                grad_rows,
                preferred_element_type=jnp.float32,
            )
        )
        d_prob = jnp.einsum(
            "bqhd,bkhd->bhqk",
            grad_rows,
            values_all[:, :last_row],
            preferred_element_type=jnp.float32,
        )
        row_delta = jnp.sum(probability * d_prob, axis=-1, keepdims=True)
        d_scores = (probability * (d_prob - row_delta)).astype(jnp.bfloat16)
        d_query_parts.append(
            jnp.einsum(
                "bhqk,bkhd->bqhd",
                d_scores,
                keys_all[:, :last_row],
                preferred_element_type=jnp.float32,
            )
            * score_scale
        )
        d_keys = d_keys.at[:, :last_row].add(
            jnp.einsum(
                "bhqk,bqhd->bkhd",
                d_scores,
                queries[:, first_row:last_row],
                preferred_element_type=jnp.float32,
            )
            * score_scale
        )
    d_queries = jnp.concatenate(d_query_parts, axis=1)
    d_heads = (
        jnp.stack([d_queries, d_keys, d_values], axis=3)
        .astype(jnp.bfloat16)
        .reshape(seqs_here, full_len, heads_here * 3 * HEAD)
    )
    d_tokens = lax.all_to_all(d_heads, "seq", split_axis=1, concat_axis=2, tiled=True).reshape(
        row_count, HEADS, 3, HEAD
    )
    _, rotate_pull = jax.vjp(lambda packed: rotate(packed, cosine, sine_part), shaped)
    d_qkv = (
        rotate_pull(d_tokens.astype(jnp.float32))[0]
        .reshape(row_count, 3 * model_width)
        .astype(jnp.bfloat16)
    )
    g_qkv_w = transpose_dot(normed_attn, d_qkv)
    g_qkv_b = jnp.sum(d_qkv.astype(jnp.float32), axis=0)
    d_attn_in = jnp.dot(d_qkv, qkv_weight.T, preferred_element_type=jnp.float32)
    dx_attn, g_gain_one, g_bias_one = norm_back(d_attn_in, unit_attn, inv_attn, ln1_gain)
    dx_mlp, g_gain_two, g_bias_two = norm_back(d_mlp_in, unit_mlp, inv_mlp, ln2_gain)
    grad_in = (gradient + dx_attn + dx_mlp).reshape(seqs_here, local_len, model_width)
    grad_terms = (
        g_gain_one,
        g_bias_one,
        g_gain_two,
        g_bias_two,
        g_qkv_w,
        g_qkv_b,
        g_dense_w,
        g_dense_b,
        g_in_w,
        g_in_b,
        g_out_w,
        g_out_b,
    )
    reduced = (
        lax.psum_scatter(grad_terms[0], ("dp", "seq"), scatter_dimension=0, tiled=True),
        lax.psum_scatter(grad_terms[1], ("dp", "seq"), scatter_dimension=0, tiled=True),
        lax.psum_scatter(grad_terms[2], ("dp", "seq"), scatter_dimension=0, tiled=True),
        lax.psum_scatter(grad_terms[3], ("dp", "seq"), scatter_dimension=0, tiled=True),
        lax.psum_scatter(grad_terms[4], ("dp", "seq"), scatter_dimension=0, tiled=True),
        lax.psum_scatter(grad_terms[5], ("dp", "seq"), scatter_dimension=0, tiled=True),
        lax.psum_scatter(grad_terms[6], ("dp", "seq"), scatter_dimension=0, tiled=True),
        lax.psum_scatter(grad_terms[7], ("dp", "seq"), scatter_dimension=0, tiled=True),
        lax.psum_scatter(grad_terms[8], ("dp", "seq"), scatter_dimension=0, tiled=True),
        lax.psum_scatter(grad_terms[9], ("dp", "seq"), scatter_dimension=0, tiled=True),
        lax.psum_scatter(grad_terms[10], ("dp", "seq"), scatter_dimension=0, tiled=True),
        lax.psum_scatter(grad_terms[11], ("dp", "seq"), scatter_dimension=0, tiled=True),
    )
    return (hidden_out, grad_in) + tuple(reduced)


def solution(mesh):
    return jax.shard_map(
        shards,
        mesh=mesh,
        in_specs=(
            P("dp", "seq", None),
            P("dp", None),
            P(),
            P(),
            P(),
            P(),
            P(),
            P(),
            P(),
            P(),
            P(),
            P(),
            P(),
            P(),
            P("dp", "seq", None),
        ),
        out_specs=(
            P("dp", "seq", None),
            P("dp", "seq", None),
            P(("dp", "seq")),
            P(("dp", "seq")),
            P(("dp", "seq")),
            P(("dp", "seq")),
            P(("dp", "seq"), None),
            P(("dp", "seq")),
            P(("dp", "seq"), None),
            P(("dp", "seq")),
            P(("dp", "seq"), None),
            P(("dp", "seq")),
            P(("dp", "seq"), None),
            P(("dp", "seq")),
        ),
        check_vma=False,
    )
```

profile of v0, /device:TPU:0, one launch (start us, length us, event | category | flops | bytes accessed | tf_op | source)
XLA Modules:
  0.0 1516.5 jit_solution(5117657675731257331)
XLA Ops:
  8.9 3.5 fusion.105
  12.4 6.0 copy.119
  18.9 9.0 reduce.49
  28.0 3.7 reshape.1432
  31.7 6.9 all-to-all-start.2
  40.0 8.3 convolution_add_fusion
  48.3 6.6 copy.107
  54.9 3.3 convert.73
  61.1 27.4 %copy.139 = bf16[1,512,3072]{1,0,2:T(2,128)(2,1)} copy(bf16[1,512,3072]{1,2,0:T(8,128)(2,1)S(1)} %bitcast.395) | data formatting | bytes 6291456 | tf_op jit(solution)/shard_map/convert_element_type | solution.py:129
  88.6 22.0 %reduce.47 = bf16[3072,512]{1,0:T(8,128)(2,1)} reduce(bf16[3072,1,512]{2,1,0:T(2,128)(2,1)} %bitcast.392, bf16[]{:T(256)} %broadcast.808), dimensions={1}, to_apply=%bitcast.380.reduce_sub_computation | reduce | bytes 6291458
  110.5 5.2 reshape.1428
  115.8 5.3 all-to-all-start
  126.8 4.0 reshape.1433
  136.2 55.2 %all-to-all-done = bf16[4,2,196608]{2,1,0:T(2,128)(2,1)} async-done(((bf16[4,2,196608]{2,1,0:T(2,128)(2,1)}), bf16[4,2,196608]{2,1,0:T(2,128)(2,1)}, u32[]{:S(2)}, u32[]{:S(2)}) %all-to-all-start) | async-done | bytes 3145760 | tf_op jit(solution)/shard_map/all_to_all | solution.py:132
  191.4 6.2 reshape.1429
  197.6 3.7 copy.132
  201.3 4.1 copy.109
  205.4 6.3 reshape.1399
  218.6 2.9 multiply_reduce_fusion.3
  234.4 5.2 fusion.129
  239.6 8.3 fusion.177
  248.0 8.1 fusion
  256.1 8.5 fusion.130
  266.5 4.8 multiply_convert_fusion.4
  271.3 2.7 fusion.122
  277.2 4.3 multiply_reduce_fusion.2
  281.5 3.6 fusion.116
  288.1 6.4 multiply_reduce_fusion.1
  294.6 7.6 multiply_convert_fusion.1
  304.3 4.5 multiply_convert_fusion.2
  315.2 12.7 fusion.181
  328.0 12.6 reduce.48
  340.6 3.5 reshape.1430
  344.1 4.3 all-to-all-start.1
  348.4 11.5 multiply_reduce_fusion
  359.9 11.9 multiply_convert_fusion
  371.8 4.7 fusion.133
  379.8 3.8 fusion.70
  383.6 4.4 fusion.48
  388.0 4.0 reshape.1431
  392.0 2.7 copy.133
  397.0 4.8 fusion.139
  403.1 8.6 fusion.71
  414.2 15.7 %copy.125 = bf16[1,2048,768]{2,0,1:T(2,128)(2,1)} copy(bf16[1,2048,768]{1,2,0:T(8,128)(2,1)} %bitcast.397) | data formatting | bytes 6291456 | tf_op jit(solution)/shard_map/convert_element_type | solution.py:244
  429.9 33.3 %reduce.50 = bf16[2048,768]{1,0:T(8,128)(2,1)} reduce(bf16[2048,1,768]{2,1,0:T(2,128)(2,1)} %bitcast.391, bf16[]{:T(256)} %broadcast.808), dimensions={1}, to_apply=%bitcast.316.reduce_sub_computation | reduce | bytes 6291458
  463.2 4.5 reshape.1434
  467.7 118.8 %all_to_all.54 = bf16[4,2,196608]{2,1,0:T(2,128)(2,1)} all-to-all(bf16[4,2,196608]{2,1,0:T(2,128)(2,1)} %reshape.1434), channel_id=1, replica_groups=mesh['dp'=8,'seq'=4] {'seq'}, dimensions={0} | all-to-all | bytes 6291456 | tf_op jit(solution)/shard_map/all_to_all | solution.py:247
  586.5 6.2 reshape.1435
  592.7 3.3 copy.126
  596.0 3.2 convert_bitcast_fusion
  599.2 6.5 copy.127
  607.5 3.6 broadcast_select_fusion
  614.6 6.9 fusion.136
  622.3 27.9 %multiply_convert_fusion.3 = (bf16[512,4096]{1,0:T(8,128)(2,1)}, f32[512,4096]{1,0:T(8,128)}, f32[512,4096]{1,0:T(8,128)}) fusion(f32[4096]{0:T(1024)S(1)} %copy-done.45, bf16[1024,4096]{1,0:T(8,128)(2,1)} %param.45, bf16[1,512,1024]{2,1,0:T(8,128)(2,1)S(1)} %copy-done.13, f32[1024]{0:T(1024)S(1)} %copy-done.49, f32[1024]{0:T(1024)S(1)} %copy-done.41, ...), kind=kOutput, calls=%fused_computation.25 | convolution fusion | flops 4436525056 | bytes 30437376 | tf_op jit(solution)/shard_map/dot_general | solution.py:169
  650.2 14.5 convert_reduce_fusion
  666.7 8.4 fusion.171
  675.4 13.4 fusion.164
  688.8 10.7 fusion.183
  699.5 7.3 fusion.182
  709.3 9.4 fusion.87
  721.4 41.4 %all-reduce.13 = (f32[1024]{0:T(1024)S(1)}, f32[1024]{0:T(1024)S(1)}, f32[1024]{0:T(1024)S(1)}, f32[1024]{0:T(1024)S(1)}, f32[3072]{0:T(1024)S(1)}, /*index=5*/f32[1024]{0:T(1024)S(1)}, f32[4096]{0:T(1024)S(1)}) all-reduce(f32[1024]{0:T(1024)S(1)} %get-tuple-element.128, ...), channel_id=2, replica_groups=mesh['dp'=8,'seq'=4] {'dp','seq'}, use_global_device_ids=true, to_apply=%region_23.24.clone | all-reduce | flops 12288 | bytes 98304
  766.3 11.3 reduce-scatter.5.cloned.1.call-done
  777.7 366.3 %reduce-scatter.9.cloned.1.call-done = f32[32,4096]{1,0:T(8,128)} async-done(((f32[1024,4096]{1,0:T(8,128)}), f32[32,4096]{1,0:T(8,128)}) %reduce-scatter.9.cloned.1.call-update) | async-done | bytes 524304 | tf_op jit(solution)/shard_map/reduce_scatter | solution.py:285
  1143.9 365.0 %reduce-scatter.11.cloned.1.call-done = f32[128,1024]{1,0:T(8,128)} async-done(((f32[4096,1024]{1,0:T(8,128)}), f32[128,1024]{1,0:T(8,128)}) %reduce-scatter.11.cloned.1.call-update) | async-done | bytes 524304 | tf_op jit(solution)/shard_map/reduce_scatter | solution.py:287
  (218 shorter events, 80.5 us)
Async XLA Ops:
  7.2 1.7 copy-start
  12.4 26.2 %copy-start.12 = (bf16[1,512,1024]{2,1,0:T(8,128)(2,1)S(1)}, bf16[1,512,1024]{2,1,0:T(8,128)(2,1)}, u32[]{:S(2)}) copy-start(bf16[1,512,1024]{2,1,0:T(8,128)(2,1)} %param.35) | copy-start | bytes 3145732
  18.9 21.1 %copy-start.42 = (f32[1024]{0:T(1024)S(1)}, f32[1024]{0:T(1024)}, u32[]{:S(2)}) copy-start(f32[1024]{0:T(1024)} %param.37) | copy-start | bytes 12292
  18.9 21.1 %copy-start.46 = (f32[3072]{0:T(1024)S(1)}, f32[3072]{0:T(1024)}, u32[]{:S(2)}) copy-start(f32[3072]{0:T(1024)} %param.42) | copy-start | bytes 36868
  18.9 21.1 %copy-start.47 = (f32[1024]{0:T(1024)S(1)}, f32[1024]{0:T(1024)}, u32[]{:S(2)}) copy-start(f32[1024]{0:T(1024)} %param.38) | copy-start | bytes 12292
  31.7 84.1 %all-to-all-start.2 = ((bf16[4,2,65536]{2,1,0:T(2,128)(2,1)}), bf16[4,2,65536]{2,1,0:T(2,128)(2,1)}, u32[]{:S(2)}, u32[]{:S(2)}) async-start(bf16[4,2,65536]{2,1,0:T(2,128)(2,1)} %reshape.1432), calls=%async_computation.2 | async-start | bytes 2097152 | tf_op jit(solution)/shard_map/all_to_all | solution.py:185
  59.1 1.6 copy-start.31
  59.1 1.6 copy-start.33
  115.8 75.6 %all-to-all-start = ((bf16[4,2,196608]{2,1,0:T(2,128)(2,1)}), bf16[4,2,196608]{2,1,0:T(2,128)(2,1)}, u32[]{:S(2)}, u32[]{:S(2)}) async-start(bf16[4,2,196608]{2,1,0:T(2,128)(2,1)} %reshape.1428), calls=%async_computation | async-start | bytes 6291456 | tf_op jit(solution)/shard_map/all_to_all | solution.py:132
  213.9 11.3 copy-start.14
  213.9 13.4 copy-start.16
  213.9 13.4 copy-start.19
  214.9 3.7 copy-start.3
  218.6 2.9 copy-start.30
  223.3 4.1 copy-start.2
  225.2 2.2 copy-start.29
  230.0 4.5 copy-start.1
  234.4 5.2 copy-start.9
  234.4 5.2 copy-start.26
  266.5 10.7 slice-start.3
  266.5 7.5 copy-start.23
  266.5 10.7 slice-start.4
  271.3 10.2 copy-start.10
  271.3 5.9 copy-start.15
  294.6 9.7 slice-start.5
  294.6 7.6 copy-start.17
  294.6 9.6 slice-start.6
  304.2 4.5 copy-start.6
  304.2 4.5 copy-start.20
  308.8 1.9 copy-start.4
  312.0 1.3 copy-start.7
  344.1 44.0 %all-to-all-start.1 = ((bf16[4,2,65536]{2,1,0:T(2,128)(2,1)}), bf16[4,2,65536]{2,1,0:T(2,128)(2,1)}, u32[]{:S(2)}, u32[]{:S(2)}) async-start(bf16[4,2,65536]{2,1,0:T(2,128)(2,1)} %reshape.1430), calls=%async_computation.1 | async-start | bytes 2097152 | tf_op jit(solution)/shard_map/all_to_all | solution.py:163
  348.3 418.0 %reduce-scatter.7.cloned.1.call-start = ((), (), s32[]{:S(2)}) async-start(), calls=%async_computation.9 | async-start | bytes 4325376 | tf_op jit(solution)/shard_map/reduce_scatter | solution.py:283
  359.9 16.7 %copy-start.18 = (bf16[1,2048,4,64]{1,3,2,0:T(8,128)(2,1)S(1)}, bf16[1,2048,4,64]{1,3,2,0:T(8,128)(2,1)}, u32[]{:S(2)}) copy-start(bf16[1,2048,4,64]{1,3,2,0:T(8,128)(2,1)} %copy-done.16) | copy-start | bytes 3145732
  371.8 4.8 copy-start.5
  371.8 6.9 copy-start.11
  371.8 11.8 slice-start
  376.5 3.3 copy-start.8
  376.5 7.0 slice-start.1
  379.8 3.8 slice-start.2
  388.0 9.0 copy-start.38
  401.9 375.8 %reduce-scatter.5.cloned.1.call-start = ((), (), s32[]{:S(2)}) async-start(), calls=%async_computation.8 | async-start | bytes 12976128 | tf_op jit(solution)/shard_map/reduce_scatter | solution.py:281
  403.1 8.6 copy-start.21
  599.2 8.3 copy-start.44
  611.2 0.7 copy-start.34
  612.1 2.5 copy-start.13
  612.1 2.5 copy-start.36
  612.1 2.5 copy-start.40
  612.2 2.5 copy-start.43
  612.2 2.5 copy-start.48
  613.0 1.7 copy-start.22
  621.5 0.7 copy-start.45
  621.5 0.7 copy-start.49
  621.6 522.4 %reduce-scatter.9.cloned.1.call-start = ((), (), s32[]{:S(2)}) async-start(), calls=%async_computation.10 | async-start | bytes 17301504 | tf_op jit(solution)/shard_map/reduce_scatter | solution.py:285
  622.3 27.9 %copy-start.27 = (bf16[1,512,1024]{2,1,0:T(8,128)(2,1)S(1)}, bf16[1,512,1024]{2,1,0:T(8,128)(2,1)}, u32[]{:S(2)}) copy-start(bf16[1,512,1024]{2,1,0:T(8,128)(2,1)} %param.49) | copy-start | bytes 3145732
  664.7 2.0 copy-start.55
  675.1 833.8 %reduce-scatter.11.cloned.1.call-start = ((), (), s32[]{:S(2)}) async-start(), calls=%async_computation.11 | async-start | bytes 17301504 | tf_op jit(solution)/shard_map/reduce_scatter | solution.py:287
  688.8 10.7 copy-start.54
  699.5 7.3 copy-start.25
  699.5 7.4 copy-start.50
  699.5 7.4 copy-start.51
  709.3 9.4 copy-start.24
  709.3 9.4 copy-start.28
  763.4 746.1 %copy-start.53 = (f32[32]{0:T(128)}, f32[32]{0:T(128)S(1)}, u32[]{:S(2)}) copy-start(f32[32]{0:T(128)S(1)} %dynamic-slice.67) | copy-start | bytes 388
  (6 other events, 3.8 us)
Sparse Core Ops, SparseCore 0:
  402.0 176.7 reduce-scatter.6
  621.7 155.9 reduce-scatter.4
  780.6 363.2 reduce-scatter.8
  1146.8 362.1 reduce-scatter.10
where the time goes:
time: 1530 us; the launch traced here: 1520 us
  waiting for transfers between devices  798 us (52%)
  matrix products  210 us (14%)
  local copies, waits for them, and re-layouts  160 us (10%)
  blocking collectives  160 us (10%)
  other arithmetic  156 us (10%)
  starting transfers between devices  16.8 us (1%)
    reduce_scatter x1, waiting for transfers between devices, shards(): lax.psum_scatter(grad_terms[8], ('dp', 'seq'), scatter_dimension=0, tiled...  366 us
    reduce_scatter x1, waiting for transfers between devices, shards(): lax.psum_scatter(grad_terms[10], ('dp', 'seq'), scatter_dimension=0, tile...  365 us
    all_to_all x1, blocking collectives, shards(): lax.all_to_all(d_heads, 'seq', split_axis=1, concat_axis=2, tiled=True)  119 us
    unnamed x8, other arithmetic  89.7 us
    unnamed x146, local copies, waits for them, and re-layouts  61.3 us
    all_to_all x1, waiting for transfers between devices, shards(): lax.all_to_all(turned, 'seq', split_axis=2, concat_axis=1, tiled=True)  55.2 us
    unnamed x1, blocking collectives  41.4 us
    dot_general x4, matrix products, transpose_dot(): lax.dot_general(left, right, (((0,), (0,)), ((), ())), preferred_element_...  33.6 us
  transfers between devices with their start and end apart: 7, of which 4 were waited for; matrix products, arithmetic and copies ran while one was open for 22% of the time, Pallas kernels for 0%

commit v1 on v0

--- a/solution.py
+++ b/solution.py
@@ -244,9 +244,10 @@
         .astype(jnp.bfloat16)
         .reshape(seqs_here, full_len, heads_here * 3 * HEAD)
     )
-    d_tokens = lax.all_to_all(d_heads, "seq", split_axis=1, concat_axis=2, tiled=True).reshape(
-        row_count, HEADS, 3, HEAD
-    )
+    d_tokens = jnp.concatenate(
+        lax.all_to_all(jnp.stack(jnp.split(d_heads, lax.axis_size("seq"), axis=1)), "seq", 0, 0),
+        axis=2,
+    ).reshape(row_count, HEADS, 3, HEAD)
     _, rotate_pull = jax.vjp(lambda packed: rotate(packed, cosine, sine_part), shaped)
     d_qkv = (
         rotate_pull(d_tokens.astype(jnp.float32))[0]

time: 1530 us -> 1490 us (0.974)
  local copies, waits for them, and re-layouts: 160 us -> 121 us
  other arithmetic: 156 us -> 119 us
  blocking collectives: 160 us -> 182 us
  waiting for transfers between devices: 798 us -> 818 us
    unnamed x8 -> x6, other arithmetic: 89.7 us -> 56.4 us
    convert_element_type x2 -> x0, local copies, waits for them, and re-layouts: 22.3 us -> none  [the longest x1 15.7 us: shards(): d_heads = jnp.stack([d_queries, d_keys, d_values], axis=3).astype(jnp.bfl...]
    all_to_all x1, blocking collectives: 119 us -> 141 us  [shards(): lax.all_to_all(jnp.stack(jnp.split(d_heads, lax.axis_size('seq'), axis=1)...]
    reduce_scatter x1, waiting for transfers between devices: 11.3 us -> 31.4 us  [shards(): lax.psum_scatter(grad_terms[4], ('dp', 'seq'), scatter_dimension=0, tiled...]
    unnamed x146 -> x142, local copies, waits for them, and re-layouts: 61.3 us -> 52.8 us
  transfers between devices with their start and end apart: 7 -> 7, of which waited for: 4 -> 4; matrix products, arithmetic and copies ran while one was open for 22% -> 17% of each run, Pallas kernels for 0% -> 0%
where the time goes in v1:
time: 1490 us; the launch traced here: 1480 us
  waiting for transfers between devices  818 us (55%)
  matrix products  211 us (14%)
  blocking collectives  182 us (12%)
  local copies, waits for them, and re-layouts  121 us (8%)
  other arithmetic  119 us (8%)
  starting transfers between devices  16.8 us (1%)
  between operations  15.1 us (1%)
    reduce_scatter x1, waiting for transfers between devices, shards(): lax.psum_scatter(grad_terms[8], ('dp', 'seq'), scatter_dimension=0, tiled...  366 us
    reduce_scatter x1, waiting for transfers between devices, shards(): lax.psum_scatter(grad_terms[10], ('dp', 'seq'), scatter_dimension=0, tile...  365 us
    all_to_all x1, blocking collectives, shards(): lax.all_to_all(jnp.stack(jnp.split(d_heads, lax.axis_size('seq'), axis=1)...  141 us
    unnamed x6, other arithmetic  56.4 us
    all_to_all x1, waiting for transfers between devices, shards(): lax.all_to_all(turned, 'seq', split_axis=2, concat_axis=1, tiled=True)  55.2 us
    unnamed x142, local copies, waits for them, and re-layouts  52.8 us
    unnamed x1, blocking collectives  41.5 us
    dot_general x4, matrix products, transpose_dot(): lax.dot_general(left, right, (((0,), (0,)), ((), ())), preferred_element_...  34.2 us
  transfers between devices with their start and end apart: 7, of which 4 were waited for; matrix products, arithmetic and copies ran while one was open for 17% of the time, Pallas kernels for 0%

profile of v1, /device:TPU:0, one launch (start us, length us, event | category | flops | bytes accessed | tf_op | source)
XLA Modules:
  0.0 1483.5 jit_solution(2382249987254178397)
XLA Ops:
  8.9 2.5 fusion.105
  11.4 3.9 copy.120
  15.8 9.0 reduce.49
  24.8 3.7 reshape.1428
  28.6 6.9 all-to-all-start.2
  36.8 8.3 convolution_add_fusion
  45.1 6.6 copy.108
  51.7 3.3 convert.72
  57.9 27.4 %copy.140 = bf16[1,512,3072]{1,0,2:T(2,128)(2,1)} copy(bf16[1,512,3072]{1,2,0:T(8,128)(2,1)S(1)} %bitcast.396) | data formatting | bytes 6291456 | tf_op jit(solution)/shard_map/convert_element_type | solution.py:129
  85.4 22.0 %reduce.47 = bf16[3072,512]{1,0:T(8,128)(2,1)} reduce(bf16[3072,1,512]{2,1,0:T(2,128)(2,1)} %bitcast.393, bf16[]{:T(256)} %broadcast.808), dimensions={1}, to_apply=%bitcast.384.reduce_sub_computation | reduce | bytes 6291458
  107.4 5.2 reshape.1424
  112.6 5.3 all-to-all-start
  123.6 4.0 reshape.1429
  133.0 55.2 %all-to-all-done = bf16[4,2,196608]{2,1,0:T(2,128)(2,1)} async-done(((bf16[4,2,196608]{2,1,0:T(2,128)(2,1)}), bf16[4,2,196608]{2,1,0:T(2,128)(2,1)}, u32[]{:S(2)}, u32[]{:S(2)}) %all-to-all-start) | async-done | bytes 3145760 | tf_op jit(solution)/shard_map/all_to_all | solution.py:132
  188.2 6.2 reshape.1425
  194.4 3.7 copy.133
  198.1 4.1 copy.110
  202.2 6.3 reshape.1396
  208.5 2.2 slice_bitcast_fusion.2
  215.4 2.9 multiply_reduce_fusion.3
  225.5 2.6 fusion.178
  230.0 2.6 copy-done.1
  232.6 5.2 fusion.129
  237.8 8.3 fusion.177
  246.1 8.1 fusion
  254.2 8.5 fusion.130
  264.7 4.8 multiply_convert_fusion.4
  269.5 2.7 fusion.122
  275.4 4.3 multiply_reduce_fusion.2
  279.7 3.5 fusion.116
  284.3 7.0 multiply_convert_fusion.2
  298.1 6.3 multiply_reduce_fusion.1
  304.4 6.4 multiply_convert_fusion.1
  310.8 2.7 fusion.134
  313.5 2.2 fusion.36
  318.9 12.7 fusion.181
  331.7 12.6 reduce.48
  344.3 3.5 reshape.1426
  347.7 4.2 all-to-all-start.1
  352.0 11.7 multiply_reduce_fusion
  363.8 11.9 multiply_convert_fusion
  375.7 4.0 fusion.133
  382.5 3.6 fusion.70
  386.1 4.3 fusion.48
  390.5 4.0 reshape.1427
  394.5 2.7 copy.134
  397.2 2.2 copy.119
  399.4 4.8 fusion.139
  404.4 8.2 fusion.71
  414.1 140.6 %all_to_all.50 = bf16[4,1,512,768]{2,3,1,0:T(8,128)(2,1)S(1)} all-to-all(bf16[4,1,512,768]{2,3,1,0:T(8,128)(2,1)S(1)} %pad_maximum_fusion.1), channel_id=1, replica_groups=mesh['dp'=8,'seq'=4] {'seq'}, dimensions={0} | all-to-all | bytes 6291456 | tf_op jit(solution)/shard_map/all_to_all | solution.py:248
  561.1 6.9 fusion.136
  568.7 27.9 %multiply_convert_fusion.3 = (bf16[512,4096]{1,0:T(8,128)(2,1)}, f32[512,4096]{1,0:T(8,128)}, f32[512,4096]{1,0:T(8,128)}) fusion(f32[4096]{0:T(1024)S(1)} %copy-done.46, bf16[1024,4096]{1,0:T(8,128)(2,1)} %param.45, bf16[1,512,1024]{2,1,0:T(8,128)(2,1)S(1)} %copy-done.13, f32[1024]{0:T(1024)S(1)} %copy-done.50, f32[1024]{0:T(1024)S(1)} %copy-done.42, ...), kind=kOutput, calls=%fused_computation.25 | convolution fusion | flops 4436525056 | bytes 30437376 | tf_op jit(solution)/shard_map/dot_general | solution.py:169
  596.7 14.5 convert_reduce_fusion
  613.1 8.9 fusion.171
  622.4 13.6 fusion.164
  636.0 10.6 fusion.183
  646.6 7.3 fusion.182
  653.9 2.3 fusion.112
  656.3 9.1 fusion.87
  665.5 2.6 fusion.91
  668.1 41.5 %all-reduce.13 = (f32[1024]{0:T(1024)S(1)}, f32[1024]{0:T(1024)S(1)}, f32[1024]{0:T(1024)S(1)}, f32[1024]{0:T(1024)S(1)}, f32[3072]{0:T(1024)S(1)}, /*index=5*/f32[1024]{0:T(1024)S(1)}, f32[4096]{0:T(1024)S(1)}) all-reduce(f32[1024]{0:T(1024)S(1)} %get-tuple-element.128, ...), channel_id=2, replica_groups=mesh['dp'=8,'seq'=4] {'dp','seq'}, use_global_device_ids=true, to_apply=%region_23.24.clone | all-reduce | flops 12288 | bytes 98304
  713.1 31.4 %reduce-scatter.5.cloned.1.call-done = f32[32,3072]{1,0:T(8,128)} async-done(((f32[1024,3072]{1,0:T(8,128)}), f32[32,3072]{1,0:T(8,128)}) %reduce-scatter.5.cloned.1.call-update) | async-done | bytes 393232 | tf_op jit(solution)/shard_map/reduce_scatter | solution.py:282
  744.6 366.4 %reduce-scatter.9.cloned.1.call-done = f32[32,4096]{1,0:T(8,128)} async-done(((f32[1024,4096]{1,0:T(8,128)}), f32[32,4096]{1,0:T(8,128)}) %reduce-scatter.9.cloned.1.call-update) | async-done | bytes 524304 | tf_op jit(solution)/shard_map/reduce_scatter | solution.py:286
  1110.9 365.0 %reduce-scatter.11.cloned.1.call-done = f32[128,1024]{1,0:T(8,128)} async-done(((f32[4096,1024]{1,0:T(8,128)}), f32[128,1024]{1,0:T(8,128)}) %reduce-scatter.11.cloned.1.call-update) | async-done | bytes 524304 | tf_op jit(solution)/shard_map/reduce_scatter | solution.py:288
  (211 shorter events, 65.2 us)
Async XLA Ops:
  7.2 1.7 copy-start
  15.3 20.2 %copy-start.12 = (bf16[1,512,1024]{2,1,0:T(8,128)(2,1)S(1)}, bf16[1,512,1024]{2,1,0:T(8,128)(2,1)}, u32[]{:S(2)}) copy-start(bf16[1,512,1024]{2,1,0:T(8,128)(2,1)} %param.35) | copy-start | bytes 3145732
  15.8 21.0 %copy-start.43 = (f32[1024]{0:T(1024)S(1)}, f32[1024]{0:T(1024)}, u32[]{:S(2)}) copy-start(f32[1024]{0:T(1024)} %param.37) | copy-start | bytes 12292
  15.8 21.0 %copy-start.47 = (f32[3072]{0:T(1024)S(1)}, f32[3072]{0:T(1024)}, u32[]{:S(2)}) copy-start(f32[3072]{0:T(1024)} %param.42) | copy-start | bytes 36868
  15.8 21.0 %copy-start.48 = (f32[1024]{0:T(1024)S(1)}, f32[1024]{0:T(1024)}, u32[]{:S(2)}) copy-start(f32[1024]{0:T(1024)} %param.38) | copy-start | bytes 12292
  28.6 84.0 %all-to-all-start.2 = ((bf16[4,2,65536]{2,1,0:T(2,128)(2,1)}), bf16[4,2,65536]{2,1,0:T(2,128)(2,1)}, u32[]{:S(2)}, u32[]{:S(2)}) async-start(bf16[4,2,65536]{2,1,0:T(2,128)(2,1)} %reshape.1428), calls=%async_computation.2 | async-start | bytes 2097152 | tf_op jit(solution)/shard_map/all_to_all | solution.py:185
  55.9 1.6 copy-start.32
  55.9 1.6 copy-start.34
  112.6 75.6 %all-to-all-start = ((bf16[4,2,196608]{2,1,0:T(2,128)(2,1)}), bf16[4,2,196608]{2,1,0:T(2,128)(2,1)}, u32[]{:S(2)}, u32[]{:S(2)}) async-start(bf16[4,2,196608]{2,1,0:T(2,128)(2,1)} %reshape.1424), calls=%async_computation | async-start | bytes 6291456 | tf_op jit(solution)/shard_map/all_to_all | solution.py:132
  210.7 11.3 copy-start.14
  210.7 14.8 copy-start.16
  210.8 14.8 copy-start.19
  211.7 3.7 copy-start.3
  215.4 2.9 copy-start.31
  220.1 3.2 copy-start.2
  223.4 2.2 copy-start.30
  228.1 4.5 copy-start.1
  232.6 5.2 copy-start.9
  232.6 5.2 copy-start.26
  264.6 10.7 slice-start.3
  264.6 7.5 copy-start.23
  264.7 10.7 slice-start.4
  269.5 10.2 copy-start.10
  269.5 5.9 copy-start.15
  284.3 7.0 copy-start.17
  291.3 1.6 copy-start.4
  294.8 1.3 copy-start.5
  304.4 6.4 copy-start.18
  310.8 2.7 copy-start.6
  315.7 1.3 copy-start.7
  347.7 42.7 %all-to-all-start.1 = ((bf16[4,2,65536]{2,1,0:T(2,128)(2,1)}), bf16[4,2,65536]{2,1,0:T(2,128)(2,1)}, u32[]{:S(2)}, u32[]{:S(2)}) async-start(bf16[4,2,65536]{2,1,0:T(2,128)(2,1)} %reshape.1426), calls=%async_computation.1 | async-start | bytes 2097152 | tf_op jit(solution)/shard_map/all_to_all | solution.py:163
  352.0 361.1 %reduce-scatter.7.cloned.1.call-start = ((), (), s32[]{:S(2)}) async-start(), calls=%async_computation.9 | async-start | bytes 4325376 | tf_op jit(solution)/shard_map/reduce_scatter | solution.py:284
  363.8 16.0 %copy-start.11 = (bf16[4,512,512]{1,2,0:T(8,128)(2,1)S(1)}, bf16[4,512,512]{1,2,0:T(8,128)(2,1)}, u32[]{:S(2)}) copy-start(bf16[4,512,512]{1,2,0:T(8,128)(2,1)} %copy-done.10) | copy-start | bytes 6291460
  375.7 5.7 copy-start.27
  375.7 10.4 slice-start
  375.7 10.4 slice-start.1
  379.8 2.7 copy-start.8
  382.5 3.6 slice-start.2
  390.5 9.0 copy-start.39
  404.3 340.3 %reduce-scatter.5.cloned.1.call-start = ((), (), s32[]{:S(2)}) async-start(), calls=%async_computation.8 | async-start | bytes 12976128 | tf_op jit(solution)/shard_map/reduce_scatter | solution.py:282
  404.3 8.2 copy-start.20
  404.4 8.2 copy-start.21
  557.6 0.7 copy-start.33
  557.6 0.7 copy-start.35
  558.6 2.5 copy-start.13
  558.6 2.5 copy-start.37
  558.6 2.5 copy-start.41
  558.6 2.5 copy-start.44
  558.6 2.5 copy-start.49
  559.4 1.7 copy-start.22
  568.0 0.7 copy-start.42
  568.0 0.7 copy-start.46
  568.0 0.7 copy-start.50
  568.0 542.9 %reduce-scatter.9.cloned.1.call-start = ((), (), s32[]{:S(2)}) async-start(), calls=%async_computation.10 | async-start | bytes 17301504 | tf_op jit(solution)/shard_map/reduce_scatter | solution.py:286
  568.7 27.9 %copy-start.28 = (bf16[1,512,1024]{2,1,0:T(8,128)(2,1)S(1)}, bf16[1,512,1024]{2,1,0:T(8,128)(2,1)}, u32[]{:S(2)}) copy-start(bf16[1,512,1024]{2,1,0:T(8,128)(2,1)} %param.49) | copy-start | bytes 3145732
  611.2 2.0 copy-start.56
  622.1 853.9 %reduce-scatter.11.cloned.1.call-start = ((), (), s32[]{:S(2)}) async-start(), calls=%async_computation.11 | async-start | bytes 17301504 | tf_op jit(solution)/shard_map/reduce_scatter | solution.py:288
  635.9 10.6 copy-start.55
  646.6 7.3 copy-start.25
  646.6 7.3 copy-start.51
  646.6 7.3 copy-start.52
  656.3 9.2 copy-start.24
  656.3 9.2 copy-start.29
  710.2 766.3 %copy-start.54 = (f32[32]{0:T(128)}, f32[32]{0:T(128)S(1)}, u32[]{:S(2)}) copy-start(f32[32]{0:T(128)S(1)} %dynamic-slice.67) | copy-start | bytes 388
  (5 other events, 3.0 us)
Sparse Core Ops, SparseCore 0:
  404.4 178.2 reduce-scatter.6
  589.3 155.2 reduce-scatter.4
  747.6 363.3 reduce-scatter.8
  1113.8 362.1 reduce-scatter.10
